TPU v7x, 32 devices: a whole 2x2x4 slice. The times are simulated.
32 devices in a mesh: cells: 8 (over y, x, core), modes: 4 (over z).
Axes of the slice: x: 2, y: 2, z: 4, core: 2. Of those that a mesh axis runs over, the one named last changes fastest.
Arguments:
- phonons: float32 [8, 8, 8, 16, 6144], P('cells', None, None, None, 'modes'), may hold values from -6 to 6
- heaters: int32 [8, 8, 8, 16], P('cells'), may hold values 0 or 1
- courant: float32 [3, 6144], P(None, 'modes'), may hold values from 0.05 to 0.3
- upwind: int32 [3, 6144], P(None, 'modes'), may hold values from 0 to 1
- relaxation: float32 [6144], P('modes'), may hold values from 0.02 to 0.4
- source: float32 [6144], P('modes'), may hold values from -6 to 6
- coupling: bfloat16 [6144, 6144], P('modes'), may hold values from -0.0390625 to 0.0390625
Outputs:
- evolved: float32 [8, 8, 8, 16, 6144], P('cells', None, None, None, 'modes')
All inputs are finite; a program needn't handle non-finite values. No bound on the sum of `heaters` on one device may be relied on, other than what follows from the above.
Results may differ from a plain program's by a relative error of at most 0.0018.
Values may be sent and summed in bfloat16 or wider, within the bound.
A program may use at most 128 MiB of HBM per device.

v0:
```python
import jax
import jax.numpy as jnp
from jax import lax
from jax.sharding import PartitionSpec as P

GY = 4
STEPS = 2


def shifted(block, axis, distance):
    devices = range(lax.axis_size(axis))
    route = [((i - distance) % len(devices), i) for i in devices]
    return lax.ppermute(block, axis, route)


def upstream(density, forward, axis):
    widths = [(0, 0)] * density.ndim
    widths[axis] = (1, 1)
    padded = jnp.pad(density, widths)
    length_axis = density.shape[axis]
    behind = lax.slice_in_dim(padded, 0, length_axis, axis=axis)
    ahead = lax.slice_in_dim(padded, 2, length_axis + 2, axis=axis)
    return jnp.where(forward, behind, ahead)


def scatter_term(rounded, coupling):
    contract = (((1,), (1,)), ((), ()))
    gathered = lax.all_gather(rounded, "modes", axis=1, tiled=True)
    return lax.dot_general(gathered, coupling, contract, preferred_element_type=jnp.float32)


def advect(density, courant, upwind, masks):
    lower_y_ok, upper_y_ok = masks
    forward_x = upwind[0] == 1
    forward_y = upwind[1] == 1
    forward_z = upwind[2] == 1
    below_x = shifted(density[-1].astype(jnp.bfloat16), "cells", GY).astype(jnp.float32)
    above_x = shifted(density[0], "cells", -GY)
    below_y = (
        shifted(density[:, -1].astype(jnp.bfloat16), "cells", 1).astype(jnp.float32) * lower_y_ok
    )
    above_y = (
        shifted(density[:, 0].astype(jnp.bfloat16), "cells", -1).astype(jnp.float32) * upper_y_ok
    )
    upstream_z = upstream(density, forward_z, 2)
    transport = courant[0] * (density - upstream(density, forward_x, 0))
    transport = transport + courant[1] * (density - upstream(density, forward_y, 1))
    transport = transport + courant[2] * (density - upstream_z)
    transport = transport.at[0].add(-courant[0] * jnp.where(forward_x, below_x, 0.0))
    transport = transport.at[-1].add(-courant[0] * jnp.where(forward_x, 0.0, above_x))
    transport = transport.at[:, 0].add(-courant[1] * jnp.where(forward_y, below_y, 0.0))
    transport = transport.at[:, -1].add(-courant[1] * jnp.where(forward_y, 0.0, above_y))
    return transport


def per_device(phonons, heaters, courant, upwind, relaxation, source, coupling):
    density = phonons[0]
    cell_count = density.shape[0] * density.shape[1] * density.shape[2]
    mode_count = density.shape[3]
    block_total = lax.axis_size("cells")
    position = (lax.axis_index("cells") + 2) % block_total
    column = position % GY
    masks = ((column != 0).astype(jnp.float32), (column != GY - 1).astype(jnp.float32))
    heating = heaters[0].astype(jnp.float32)[..., None] * source
    for repeat in range(STEPS):
        rounded = density.astype(jnp.bfloat16).reshape(cell_count, mode_count)
        scattered = scatter_term(rounded, coupling).reshape(density.shape)
        transport = advect(density, courant, upwind, masks)
        density = density - transport - relaxation * density - scattered + heating
    return density[None]


def solution(mesh):
    placed = (
        P("cells", None, None, None, "modes"),
        P("cells", None, None, None),
        P(None, "modes"),
        P(None, "modes"),
        P("modes"),
        P("modes"),
        P("modes", None),
    )
    return jax.shard_map(
        per_device,
        mesh=mesh,
        in_specs=placed,
        out_specs=P("cells", None, None, None, "modes"),
        check_vma=False,
    )
```

profile of v0, /device:TPU:0, one launch (start us, length us, event | category | flops | bytes accessed | tf_op | source)
XLA Modules:
  0.0 519.6 jit_solution(12201974563363240435)
XLA Ops:
  6.5 5.0 convert.12
  11.5 0.0 all-gather.3.cloned.1.call-update
  11.6 0.0 all-gather.5.cloned.1.call-start
  11.6 1.0 slice_bitcast_fusion.10
  12.6 0.0 copy-start.18
  12.6 0.0 copy-start.17
  12.7 0.0 slice-start
  12.7 3.0 collective-permute-start
  15.7 1.2 slice_bitcast_fusion.4
  16.9 0.0 slice-start.1
  16.9 0.2 collective-permute-start.1
  17.2 3.4 copy.37
  20.6 0.1 slice_bitcast_fusion.8
  20.6 0.1 collective-permute-start.2
  20.7 2.6 collective-permute-start.3
  23.3 0.1 slice_reduce_fusion.2
  23.4 0.1 compare_reduce_fusion.2
  23.5 7.2 %fusion.4 = f32[8,8,16,1536]{3,2,1,0:T(8,128)} fusion(f32[8,8,16,1536]{3,2,1,0:T(8,128)S(1)} %bitcast.82, f32[1536]{0:T(1024)S(1)} %get-tuple-element.105, f32[1536]{0:T(1024)S(1)} %get-tuple-element.106, f32[1536]{0:T(1024)S(1)} %get-tuple-element.104, pred[1536]{0:T(1024)(128)(4,1)S(1)} %get-tuple-element.102, pred[1536]{0:T(1024)(128)(4,1)S(1)} %get-tuple-element.103, ...), kind=kLoop, calls=%fused_computation.18 | loop fusion | flops 17301504 | bytes 12605952 | tf_op jit(solution)/shard_map/add | solution.py:48
  30.7 0.0 copy-done.3
  30.7 0.0 copy-done.5
  30.8 0.7 neg.21
  31.5 1.4 convert_bitcast_fusion
  32.9 0.0 collective-permute-done
  32.9 2.3 fusion.35
  35.2 6.2 %copy.16 = f32[8,8,16,1536]{3,2,0,1:T(8,128)} copy(f32[8,8,16,1536]{3,2,1,0:T(8,128)} %fusion.35) | data formatting | bytes 12582912 | tf_op jit(solution)/shard_map/scatter-add | solution.py:49
  41.4 4.5 collective-permute-done.1
  45.9 0.0 copy-done.9
  45.9 2.2 fusion.34
  48.0 0.0 collective-permute-done.2
  48.1 0.0 copy-done.6
  48.1 2.2 fusion.32
  50.3 0.0 collective-permute-done.3
  50.3 2.1 fusion.31
  52.4 180.2 %all-gather.3.cloned.1.call-done = bf16[1024,6144]{1,0:T(8,128)(2,1)} async-done(((bf16[1024,1536]{1,0:T(8,128)(2,1)}), bf16[1024,6144]{1,0:T(8,128)(2,1)}) %all-gather.3.cloned.1.call-update) | async-done | bytes 12582928 | tf_op jit(solution)/shard_map/all_gather | solution.py:28
  232.6 24.1 %fusion.37 = f32[1024,1536]{1,0:T(8,128)S(1)} fusion(bf16[1024,6144]{1,0:T(8,128)(2,1)} %all-gather.3.cloned.1.call-done, bf16[1536,6144]{1,0:T(8,128)(2,1)} %param.29), kind=kOutput, calls=%fused_computation.77 | convolution fusion | flops 19327352832 | bytes 37748736 | tf_op jit(solution)/shard_map/dot_general | solution.py:29
  256.7 0.0 copy-done
  256.7 0.0 copy-done.13
  256.7 0.0 copy-done.14
  256.8 0.0 copy-start.2
  256.8 0.0 copy-start.4
  256.8 0.0 copy-start.7
  256.8 8.1 %fusion.36 = (bf16[8,8,16,1536]{3,2,1,0:T(8,128)(2,1)}, f32[8,8,16,1536]{3,2,1,0:T(8,128)}) fusion(f32[1536]{0:T(1024)S(1)} %copy-done.13, f32[8,8,16]{2,1,0:T(8,128)S(1)} %copy-done, f32[8,8,16,1536]{3,2,0,1:T(8,128)} %fusion.31, f32[8,8,16,1536]{3,2,1,0:T(8,128)S(1)} %bitcast.86, f32[1,8,8,16,1536]{4,3,2,1,0:T(8,128)} %param.23, f32[1536]{0:T(1024)S(1)} %copy-done.14), kind=kLoop, calls=%fused_computation.76 | loop fusion | flops 11010048 | bytes 28327936 | tf_op jit(solution)/shard_map/convert.2
  264.9 0.0 all-gather.5.cloned.1.call-update
  265.0 1.0 slice_bitcast_fusion.7
  266.0 1.5 collective-permute-start.4
  267.5 1.2 slice_bitcast_fusion.1
  268.7 0.6 collective-permute-start.5
  269.4 18.0 %fusion.12 = f32[8,8,16,1536]{3,2,1,0:T(8,128)S(1)} fusion(f32[8,8,16,1536]{3,2,1,0:T(8,128)} %get-tuple-element.108, f32[1536]{0:T(1024)S(1)} %copy-done.12, f32[1536]{0:T(1024)S(1)} %copy-done.4, f32[1536]{0:T(1024)S(1)} %copy-done.2, pred[1536]{0:T(1024)(128)(4,1)S(1)} %copy-done.16, pred[1536]{0:T(1024)(128)(4,1)S(1)} %copy-done.7, ...), kind=kLoop, calls=%fused_computation.26 | loop fusion | flops 17301504 | bytes 12605952 | tf_op jit(solution)/shard_map/add | solution.py:48
  287.4 1.2 slice_bitcast_fusion.5
  288.6 0.2 collective-permute-start.6
  288.8 2.6 collective-permute-start.7
  291.5 0.0 collective-permute-done.4
  291.5 0.2 fusion.30
  291.7 0.8 copy.20
  292.5 4.6 collective-permute-done.5
  297.1 0.1 fusion.29
  297.2 2.1 collective-permute-done.6
  299.3 0.3 fusion.27
  299.5 3.0 copy.22
  302.6 0.0 collective-permute-done.7
  302.6 1.1 fusion.26
  303.6 177.9 %all-gather.5.cloned.1.call-done = bf16[1024,6144]{1,0:T(8,128)(2,1)} async-done(((bf16[1024,1536]{1,0:T(8,128)(2,1)}), bf16[1024,6144]{1,0:T(8,128)(2,1)}) %all-gather.5.cloned.1.call-update) | async-done | bytes 12582928 | tf_op jit(solution)/shard_map/all_gather | solution.py:28
  481.5 24.1 %fusion.38 = f32[1024,1536]{1,0:T(8,128)S(1)} fusion(bf16[1024,6144]{1,0:T(8,128)(2,1)} %all-gather.5.cloned.1.call-done, bf16[1536,6144]{1,0:T(8,128)(2,1)} %param.29), kind=kOutput, calls=%fused_computation.78 | convolution fusion | flops 19327352832 | bytes 37748736 | tf_op jit(solution)/shard_map/dot_general | solution.py:29
  505.6 7.1 %fusion.16 = f32[1,8,8,16,1536]{4,3,2,1,0:T(8,128)} fusion(f32[8,8,16,1536]{3,2,1,0:T(8,128)S(1)} %bitcast.85, f32[8,8,16,1536]{3,2,1,0:T(8,128)} %get-tuple-element.108, f32[8,8,16,1536]{3,2,1,0:T(8,128)} %fusion.26, f32[1536]{0:T(1024)S(1)} %copy-done.14, f32[1536]{0:T(1024)S(1)} %copy-done.13, f32[8,8,16]{2,1,0:T(8,128)S(1)} %copy-done), kind=kLoop, calls=%fused_computation.30 | loop fusion | flops 9437184 | bytes 25182208 | tf_op jit(solution)/shard_map/broadcast_in_dim | solution.py:70
  (31 shorter events, 0.1 us)
Async XLA Ops:
  6.5 226.1 %all-gather.3.cloned.1.call-start = ((), (), s32[]{:S(2)}) async-start(), calls=%async_computation | async-start | bytes 15728640 | tf_op jit(solution)/shard_map/all_gather | solution.py:28
  11.6 469.9 %all-gather.5.cloned.1.call-start = ((), (), s32[]{:S(2)}) async-start(), calls=%async_computation.1 | async-start | bytes 15728640 | tf_op jit(solution)/shard_map/all_gather | solution.py:28
  12.6 10.7 %copy-start.18 = (f32[3,1536]{1,0:T(4,128)S(1)}, f32[3,1536]{1,0:T(4,128)}, u32[]{:S(2)}) copy-start(f32[3,1536]{1,0:T(4,128)} %param.25) | copy-start | bytes 55300
  12.6 10.7 %copy-start.17 = (s32[3,1536]{1,0:T(4,128)S(1)}, s32[3,1536]{1,0:T(4,128)}, u32[]{:S(2)}) copy-start(s32[3,1536]{1,0:T(4,128)} %param.26) | copy-start | bytes 55300
  12.7 10.9 %slice-start = ((s8[6291456]{0:T(1024)(128)(4,1)}), s8[4194304]{0:T(1024)(128)(4,1)S(1)}, s32[]{:S(2)}) async-start(s8[6291456]{0:T(1024)(128)(4,1)} %bitcast.80), calls=%async_computation.2 | async-start | bytes 8388608
  12.7 20.2 %collective-permute-start = (bf16[8,16,1536]{2,1,0:T(8,128)(2,1)S(1)}, bf16[8,16,1536]{2,1,0:T(8,128)(2,1)}, u32[]{:S(2)}, u32[]{:S(2)}) collective-permute-start(bf16[8,16,1536]{2,1,0:T(8,128)(2,1)S(1)} %slice_bitcast_fusion.10), channel_id=1, source_target_pairs={{16,0},{20,4},{24,8},{28,12},{0,16},{4,20},{8,24},{12,28},{17,1},{... | collective-permute-start | bytes 1179656 | tf_op jit(solution)/shard_map/ppermute | solution.py:13
  16.9 6.6 %slice-start.1 = ((s8[6291456]{0:T(1024)(128)(4,1)}), s8[2097152]{0:T(1024)(128)(4,1)S(1)}, s32[]{:S(2)}) async-start(s8[6291456]{0:T(1024)(128)(4,1)} %bitcast.80), calls=%async_computation.3 | async-start | bytes 4194304
  16.9 29.0 %collective-permute-start.1 = (f32[8,16,1536]{2,1,0:T(8,128)S(1)}, f32[8,16,1536]{2,1,0:T(8,128)S(1)}, u32[]{:S(2)}, u32[]{:S(2)}) collective-permute-start(f32[8,16,1536]{2,1,0:T(8,128)S(1)} %slice_bitcast_fusion.4), channel_id=1, source_target_pairs={{16,0},{20,4},{24,8},{28,12},{0,16},{4,20},{8,24},{12,28},{17,1},{... | collective-permute-start | bytes 2359304 | tf_op jit(solution)/shard_map/ppermute | solution.py:13
  20.6 27.4 %collective-permute-start.2 = (bf16[8,16,1536]{2,1,0:T(8,128)(2,1)S(1)}, bf16[8,16,1536]{2,1,0:T(8,128)(2,1)S(1)}, u32[]{:S(2)}, u32[]{:S(2)}) collective-permute-start(bf16[8,16,1536]{2,1,0:T(8,128)(2,1)S(1)} %get-tuple-element.112), channel_id=1, source_target_pairs={{28,0},{0,4},{4,8},{8,12},{12,16},{16,20},{20,24},{24,28},{29,1},{... | collective-permute-start | bytes 1179656 | tf_op jit(solution)/shard_map/ppermute | solution.py:13
  20.7 29.6 %collective-permute-start.3 = (bf16[8,16,1536]{2,1,0:T(8,128)(2,1)S(1)}, bf16[8,16,1536]{2,1,0:T(8,128)(2,1)S(1)}, u32[]{:S(2)}, u32[]{:S(2)}) collective-permute-start(bf16[8,16,1536]{2,1,0:T(8,128)(2,1)S(1)} %get-tuple-element.111), channel_id=1, source_target_pairs={{4,0},{8,4},{12,8},{16,12},{20,16},{24,20},{28,24},{0,28},{5,1},{9... | collective-permute-start | bytes 1179656 | tf_op jit(solution)/shard_map/ppermute | solution.py:13
  23.4 7.4 %copy-start.3 = (f32[1536]{0:T(1024)}, f32[1536]{0:T(1024)S(1)}, u32[]{:S(2)}) copy-start(f32[1536]{0:T(1024)S(1)} %get-tuple-element.106) | copy-start | bytes 18436
  23.4 7.4 %copy-start.11 = (f32[1536]{0:T(1024)}, f32[1536]{0:T(1024)S(1)}, u32[]{:S(2)}) copy-start(f32[1536]{0:T(1024)S(1)} %get-tuple-element.105) | copy-start | bytes 18436
  23.4 7.4 %copy-start.1 = (f32[1536]{0:T(1024)}, f32[1536]{0:T(1024)S(1)}, u32[]{:S(2)}) copy-start(f32[1536]{0:T(1024)S(1)} %get-tuple-element.104) | copy-start | bytes 18436
  23.5 7.3 %copy-start.5 = (pred[1536]{0:T(1024)(128)(4,1)}, pred[1536]{0:T(1024)(128)(4,1)S(1)}, u32[]{:S(2)}) copy-start(pred[1536]{0:T(1024)(128)(4,1)S(1)} %get-tuple-element.103) | copy-start | bytes 4612
  23.5 7.3 %copy-start.8 = (pred[1536]{0:T(1024)(128)(4,1)}, pred[1536]{0:T(1024)(128)(4,1)S(1)}, u32[]{:S(2)}) copy-start(pred[1536]{0:T(1024)(128)(4,1)S(1)} %get-tuple-element.101) | copy-start | bytes 4612
  23.5 7.3 %copy-start.15 = (pred[1536]{0:T(1024)(128)(4,1)}, pred[1536]{0:T(1024)(128)(4,1)S(1)}, u32[]{:S(2)}) copy-start(pred[1536]{0:T(1024)(128)(4,1)S(1)} %get-tuple-element.102) | copy-start | bytes 4612
  35.2 10.7 %copy-start.9 = (pred[1536]{0:T(1024)(128)(4,1)S(1)}, pred[1536]{0:T(1024)(128)(4,1)}, u32[]{:S(2)}) copy-start(pred[1536]{0:T(1024)(128)(4,1)} %copy-done.8) | copy-start | bytes 4612
  35.2 12.9 %copy-start.6 = (pred[1536]{0:T(1024)(128)(4,1)S(1)}, pred[1536]{0:T(1024)(128)(4,1)}, u32[]{:S(2)}) copy-start(pred[1536]{0:T(1024)(128)(4,1)} %copy-done.5) | copy-start | bytes 4612
  52.4 204.3 %copy-start = (f32[8,8,16]{2,1,0:T(8,128)S(1)}, f32[8,8,16]{2,1,0:T(8,128)}, u32[]{:S(2)}) copy-start(f32[8,8,16]{2,1,0:T(8,128)} %convert_bitcast_fusion) | copy-start | bytes 12292
  52.4 204.3 %copy-start.13 = (f32[1536]{0:T(1024)S(1)}, f32[1536]{0:T(1024)}, u32[]{:S(2)}) copy-start(f32[1536]{0:T(1024)} %param.28) | copy-start | bytes 18436
  52.4 204.3 %copy-start.14 = (f32[1536]{0:T(1024)S(1)}, f32[1536]{0:T(1024)}, u32[]{:S(2)}) copy-start(f32[1536]{0:T(1024)} %param.27) | copy-start | bytes 18436
  256.8 12.6 %copy-start.2 = (f32[1536]{0:T(1024)S(1)}, f32[1536]{0:T(1024)}, u32[]{:S(2)}) copy-start(f32[1536]{0:T(1024)} %copy-done.1) | copy-start | bytes 18436
  256.8 12.6 %copy-start.4 = (f32[1536]{0:T(1024)S(1)}, f32[1536]{0:T(1024)}, u32[]{:S(2)}) copy-start(f32[1536]{0:T(1024)} %copy-done.3) | copy-start | bytes 18436
  256.8 12.6 %copy-start.7 = (pred[1536]{0:T(1024)(128)(4,1)S(1)}, pred[1536]{0:T(1024)(128)(4,1)}, u32[]{:S(2)}) copy-start(pred[1536]{0:T(1024)(128)(4,1)} %copy-done.5) | copy-start | bytes 4612
  256.8 12.6 %copy-start.10 = (pred[1536]{0:T(1024)(128)(4,1)S(1)}, pred[1536]{0:T(1024)(128)(4,1)}, u32[]{:S(2)}) copy-start(pred[1536]{0:T(1024)(128)(4,1)} %copy-done.8) | copy-start | bytes 4612
  256.8 12.6 %copy-start.12 = (f32[1536]{0:T(1024)S(1)}, f32[1536]{0:T(1024)}, u32[]{:S(2)}) copy-start(f32[1536]{0:T(1024)} %copy-done.11) | copy-start | bytes 18436
  256.8 12.6 %copy-start.16 = (pred[1536]{0:T(1024)(128)(4,1)S(1)}, pred[1536]{0:T(1024)(128)(4,1)}, u32[]{:S(2)}) copy-start(pred[1536]{0:T(1024)(128)(4,1)} %copy-done.15) | copy-start | bytes 4612
  266.0 25.5 %collective-permute-start.4 = (bf16[8,16,1536]{2,1,0:T(8,128)(2,1)S(1)}, bf16[8,16,1536]{2,1,0:T(8,128)(2,1)S(1)}, u32[]{:S(2)}, u32[]{:S(2)}) collective-permute-start(bf16[8,16,1536]{2,1,0:T(8,128)(2,1)S(1)} %slice_bitcast_fusion.7), channel_id=1, source_target_pairs={{16,0},{20,4},{24,8},{28,12},{0,16},{4,20},{8,24},{12,28},{17,1},{... | collective-permute-start | bytes 1179656 | tf_op jit(solution)/shard_map/ppermute | solution.py:13
  268.7 28.4 %collective-permute-start.5 = (f32[8,16,1536]{2,1,0:T(8,128)S(1)}, f32[8,16,1536]{2,1,0:T(8,128)S(1)}, u32[]{:S(2)}, u32[]{:S(2)}) collective-permute-start(f32[8,16,1536]{2,1,0:T(8,128)S(1)} %slice_bitcast_fusion.1), channel_id=1, source_target_pairs={{16,0},{20,4},{24,8},{28,12},{0,16},{4,20},{8,24},{12,28},{17,1},{... | collective-permute-start | bytes 2359304 | tf_op jit(solution)/shard_map/ppermute | solution.py:13
  288.6 10.7 %collective-permute-start.6 = (bf16[8,16,1536]{2,1,0:T(8,128)(2,1)S(1)}, bf16[8,16,1536]{2,1,0:T(8,128)(2,1)S(1)}, u32[]{:S(2)}, u32[]{:S(2)}) collective-permute-start(bf16[8,16,1536]{2,1,0:T(8,128)(2,1)S(1)} %get-tuple-element.110), channel_id=1, source_target_pairs={{28,0},{0,4},{4,8},{8,12},{12,16},{16,20},{20,24},{24,28},{29,1},{... | collective-permute-start | bytes 1179656 | tf_op jit(solution)/shard_map/ppermute | solution.py:13
  288.8 13.7 %collective-permute-start.7 = (bf16[8,16,1536]{2,1,0:T(8,128)(2,1)S(1)}, bf16[8,16,1536]{2,1,0:T(8,128)(2,1)S(1)}, u32[]{:S(2)}, u32[]{:S(2)}) collective-permute-start(bf16[8,16,1536]{2,1,0:T(8,128)(2,1)S(1)} %get-tuple-element.109), channel_id=1, source_target_pairs={{4,0},{8,4},{12,8},{16,12},{20,16},{24,20},{28,24},{0,28},{5,1},{9... | collective-permute-start | bytes 1179656 | tf_op jit(solution)/shard_map/ppermute | solution.py:13
Sparse Core Ops, SparseCore 0:
  11.7 220.8 all-gather.2
  265.1 216.3 all-gather.4
where the time goes:
time: 520 us
  waiting for transfers between devices  369 us (71%)
  other arithmetic  58.1 us (11%)
  matrix products  48.2 us (9%)
  local copies, waits for them, and re-layouts  19.2 us (4%)
  between operations  13.8 us (3%)
  starting transfers between devices  11 us (2%)
    all_gather x2, waiting for transfers between devices, scatter_term(): gathered = lax.all_gather(rounded, 'modes', axis=1, tiled=True)  358 us
    dot_general x2, matrix products, scatter_term(): lax.dot_general(gathered, coupling, contract, preferred_element_type=jnp....  48.2 us
    add x2, other arithmetic, advect(): transport = transport + courant[2] * (density - upstream_z)  25.2 us
    another operation x2, other arithmetic  13.1 us
    ppermute x8, waiting for transfers between devices, shifted(): return lax.ppermute(block, axis, route)  11.2 us
    ppermute x8, starting transfers between devices, shifted(): return lax.ppermute(block, axis, route)  11 us
  transfers between devices with their start and end apart: 10, of which 5 were waited for; matrix products, arithmetic and copies ran while one was open for 11% of the time, Pallas kernels for 0%

commit v1 on v0

--- a/solution.py
+++ b/solution.py
@@ -1,10 +1,321 @@
 import jax
 import jax.numpy as jnp
 from jax import lax
+from jax.experimental import pallas as pl
+from jax.experimental.pallas import tpu as pltpu
 from jax.sharding import PartitionSpec as P
 
 GY = 4
 STEPS = 2
+
+PLANES = 1
+TILE = 256
+LENT_AT = 5
+MESH = pl.DeviceIdType.MESH
+
+
+def line_kernel(phonons, heat, rates, coupling, out, dens, own, got, weights, old, facex, facey, total,
+                load_sem, ss, rs, fys, fyr, fxs, fxr, hs, hr, out_sem):
+    cell, me = lax.axis_index("cells"), lax.axis_index("modes")
+    count = own.shape[0]
+    steps_all = STEPS * count
+    planes = count * PLANES
+    ny, nz, width = own.shape[2:]
+    rows = PLANES * ny * nz
+    blocks = lax.axis_size("cells")
+    half = me // 2
+    inner = lax.rem((me + 1) // 2, 2)
+    is_inner = inner == 1
+    toward = 1 - 2 * half
+    inward, outward = me + toward, me - toward
+    near, far = me + 2 * toward, 3 - 3 * half
+    y_next, y_last = lax.rem(cell + 1, blocks), lax.rem(cell + blocks - 1, blocks)
+    x_next, x_last = lax.rem(cell + GY, blocks), lax.rem(cell + blocks - GY, blocks)
+    twin = cell + 1 - 2 * lax.rem(cell, 2)
+    flip2 = 2 - 4 * lax.rem(cell // 2, 2)
+    flip4 = 4 - 8 * lax.rem(cell // 4, 2)
+    peers = (cell + flip2, cell + flip4, cell + flip2 + flip4)
+    column = lax.rem(lax.rem(cell + 2, blocks), GY)
+    low_ok = jnp.where(column != 0, 1.0, 0.0).astype(jnp.float32)
+    high_ok = jnp.where(column != GY - 1, 1.0, 0.0).astype(jnp.float32)
+
+    def remote(src, dst, send, recv, c, m):
+        return pltpu.make_async_remote_copy(
+            src_ref=src, dst_ref=dst, send_sem=send, recv_sem=recv, device_id=(c, m), device_id_type=MESH
+        )
+
+    def own_in(i):
+        return remote(own.at[lax.rem(i, count)], got.at[1 - inner, i], ss.at[0, i], rs.at[1 - inner, i], cell, inward)
+
+    def own_out(i):
+        return remote(own.at[lax.rem(i, count)], got.at[0, i], ss.at[1, i], rs.at[0, i], cell, outward)
+
+    def relay(i):
+        return remote(got.at[1, i], got.at[2, i], ss.at[2, i], rs.at[2, i], cell, inward)
+
+    def part(i):
+        return remote(got.at[1, i], got.at[2, i], ss.at[3, i], rs.at[2, i], cell, outward)
+
+    def arrived(slot, i):
+        remote(got.at[slot, i], got.at[slot, i], ss.at[0, i], rs.at[slot, i], cell, inward).wait_recv()
+
+    def face_y(side, i):
+        line = own.at[lax.rem(i, count), :, ny - 1 if side == 0 else 0]
+        return remote(line, facey.at[side, i], fys.at[side, i], fyr.at[side, i], y_next if side == 0 else y_last, me)
+
+    def face_x(side, s):
+        plane = own.at[count - 1, PLANES - 1] if side == 0 else own.at[0, 0]
+        return remote(plane, facex.at[side, s], fxs.at[side, s], fxr.at[side, s], x_next if side == 0 else x_last, me)
+
+    share = width // blocks
+
+    def lent_rows(c):
+        return pl.ds(pl.multiple_of(c * share, share), share)
+
+    def lent_z(k):
+        block = near if k == 0 else far
+        src = coupling.at[lent_rows(cell), pl.ds(pl.multiple_of(block * width, width), width)]
+        return remote(src, weights.at[4 + k, lent_rows(cell)], hs.at[k], hr.at[k], cell, inward)
+
+    def lent_peer(q, k):
+        piece = weights.at[4 + k, lent_rows(cell)]
+        return remote(piece, piece, hs.at[2 + 2 * q + k], hr.at[2 + 2 * q + k], peers[q], me)
+
+    def lent_twin(q, k):
+        piece = weights.at[4 + k, lent_rows(cell if q == 3 else peers[q])]
+        return remote(piece, piece, hs.at[8 + 2 * q + k], hr.at[8 + 2 * q + k], twin, me)
+
+    pairs = [(q, k) for q in range(3) for k in range(2)]
+    twins = [(q, k) for q in range(4) for k in range(2)]
+
+    def on_own_sends(i, act):
+        act(own_in(i))
+        pl.when(is_inner)(lambda: act(own_out(i)))
+        act(face_y(0, i))
+        act(face_y(1, i))
+        pl.when(lax.rem(i, count) == 0)(lambda: act(face_x(1, i // count)))
+        pl.when(lax.rem(i, count) == count - 1)(lambda: act(face_x(0, i // count)))
+
+    def matrix(piece):
+        return piece[...].reshape(rows, width)
+
+    def product(piece, block, tile):
+        weight = weights[block, pl.ds(pl.multiple_of(tile * TILE, TILE), TILE), :]
+        return lax.dot_general(matrix(piece), weight, (((1,), (1,)), ((), ())), preferred_element_type=jnp.float32)
+
+    def add_product(piece, block, first=False):
+        @pl.loop(0, width // TILE)
+        def _(tile):
+            lanes = pl.ds(pl.multiple_of(tile * TILE, TILE), TILE)
+            value = product(piece, block, tile)
+            total[:, lanes] = value if first else total[:, lanes] + value
+
+    def partial_sum(i):
+        relay(i).wait_send()
+
+        @pl.loop(0, width // TILE)
+        def _(tile):
+            lanes = pl.ds(pl.multiple_of(tile * TILE, TILE), TILE)
+            value = product(got.at[0, i], 4, tile) + product(got.at[2, i], 5, tile)
+            got[1, i, :, :, :, lanes] = value.astype(jnp.bfloat16).reshape(PLANES, ny, nz, TILE)
+
+        part(i).start()
+
+    def process(i):
+        s, k = i // count, lax.rem(i, count)
+        add_product(own.at[k], 0, True)
+        arrived(0, i)
+        add_product(got.at[0, i], 1)
+        pl.when(is_inner)(lambda: add_product(got.at[1, i], 2))
+        arrived(2, i)
+        pl.when(is_inner)(lambda: add_product(got.at[2, i], 3))
+
+        @pl.when(jnp.logical_not(is_inner))
+        def _():
+            total[...] = total[...] + got[2, i].reshape(rows, width).astype(jnp.float32)
+
+        face_y(0, i).wait_recv()
+        face_y(1, i).wait_recv()
+
+        @pl.when(k == 0)
+        def _():
+            face_x(0, s).wait_recv()
+            old[1, 1 : ny + 1] = facex[0, s].astype(jnp.float32)
+
+        @pl.when(k == count - 1)
+        def _():
+            face_x(1, s).wait_recv()
+            dens[planes] = facex[1, s].astype(jnp.float32)
+
+        on_own_sends(i, lambda copy: copy.wait_send())
+        spot = lax.broadcasted_iota(jnp.int32, (nz, 512), 0)
+        for p in range(PLANES):
+            plane = k * PLANES + p
+            cur = lax.rem(plane, 2)
+            old[cur, 1 : ny + 1] = dens[plane]
+            old[cur, 0] = facey[0, i, p].astype(jnp.float32) * low_ok
+            old[cur, ny + 1] = facey[1, i, p].astype(jnp.float32) * high_ok
+
+            @pl.loop(0, ny)
+            def _(y):
+                warm = heat[plane, pl.ds(pl.multiple_of(y * nz, nz), nz), :]
+                for lane in range(0, width, 512):
+                    lanes = slice(lane, lane + 512)
+                    here = old[cur, y + 1, :, lanes]
+                    new = rates[0:1, lanes] * here
+                    new += rates[1:2, lanes] * old[1 - cur, y + 1, :, lanes]
+                    new += rates[2:3, lanes] * dens[plane + 1, y, :, lanes]
+                    new += rates[3:4, lanes] * old[cur, y, :, lanes]
+                    new += rates[4:5, lanes] * old[cur, y + 2, :, lanes]
+                    new += rates[5:6, lanes] * jnp.where(spot == 0, 0.0, pltpu.roll(here, 1, 0))
+                    new += rates[6:7, lanes] * jnp.where(spot == nz - 1, 0.0, pltpu.roll(here, nz - 1, 0))
+                    line = pl.ds(pl.multiple_of((p * ny + y) * nz, nz), nz)
+                    new += warm * rates[7:8, lanes] - total[line, lanes]
+                    dens[plane, y, :, lanes] = new
+                    own[k, p, y, :, lanes] = new.astype(jnp.bfloat16)
+
+        pl.when(s < STEPS - 1)(lambda: on_own_sends(i + count, lambda copy: copy.start()))
+        pl.when(s == STEPS - 1)(lambda: result(k).start())
+
+    def result(k):
+        span = pl.ds(k * PLANES, PLANES)
+        return pltpu.make_async_copy(dens.at[span], out.at[0, span], out_sem.at[k])
+
+    load_density = pltpu.make_async_copy(phonons.at[0], dens.at[pl.ds(0, planes)], load_sem.at[4])
+    load_density.start()
+    order = (me, inward, jnp.clip(outward, 0, 3), far)
+    loads = [
+        pltpu.make_async_copy(
+            coupling.at[:, pl.ds(pl.multiple_of(block * width, width), width)], weights.at[j], load_sem.at[j]
+        )
+        for j, block in enumerate(order)
+    ]
+    for load in loads:
+        load.start()
+
+    barrier = pltpu.get_barrier_semaphore()
+
+    def greet(c, m):
+        pl.semaphore_signal(barrier, inc=1, device_id=(c, m), device_id_type=MESH)
+
+    greet(cell, inward)
+    pl.when(is_inner)(lambda: greet(cell, outward))
+    for c in (y_next, y_last, x_next, x_last, twin) + peers:
+        greet(c, me)
+    pl.semaphore_wait(barrier, 9 + inner)
+
+    @pl.when(jnp.logical_not(is_inner))
+    def _():
+        lent_z(0).start()
+        lent_z(1).start()
+
+    load_density.wait()
+
+    @pl.loop(0, count)
+    def _(i):
+        own[i] = dens[pl.ds(i * PLANES, PLANES)].astype(jnp.bfloat16)
+        on_own_sends(i, lambda copy: copy.start())
+
+    for load in loads:
+        load.wait()
+
+    @pl.loop(0, steps_all + 1)
+    def _(t):
+        @pl.when(is_inner)
+        def _():
+            @pl.when(t < steps_all)
+            def _():
+                arrived(1, t)
+                relay(t).start()
+
+            @pl.when(t == LENT_AT - 3)
+            def _():
+                for k in range(2):
+                    lent_z(k).wait_recv()
+                for q, k in pairs:
+                    lent_peer(q, k).start()
+
+            @pl.when(t == LENT_AT - 1)
+            def _():
+                for q, k in pairs:
+                    lent_peer(q, k).wait_recv()
+                for q, k in twins:
+                    lent_twin(q, k).start()
+
+        @pl.when(t >= 1)
+        def _():
+            u = t - 1
+            process(u)
+
+            @pl.when(is_inner)
+            def _():
+                @pl.when(u == LENT_AT)
+                def _():
+                    for q, k in twins:
+                        lent_twin(q, k).wait_recv()
+                    pl.loop(0, LENT_AT)(partial_sum)
+
+                pl.when(u >= LENT_AT)(lambda: partial_sum(u))
+
+    @pl.loop(0, count)
+    def _(k):
+        result(k).wait()
+
+    @pl.when(is_inner)
+    def _():
+        pl.loop(0, steps_all)(lambda i: part(i).wait_send())
+        for q, k in pairs:
+            lent_peer(q, k).wait_send()
+        for q, k in twins:
+            lent_twin(q, k).wait_send()
+
+    @pl.when(jnp.logical_not(is_inner))
+    def _():
+        lent_z(0).wait_send()
+        lent_z(1).wait_send()
+
+
+def line_device(phonons, heaters, courant, upwind, relaxation, source, coupling):
+    _, planes, ny, nz, width = phonons.shape
+    count = planes // PLANES
+    calls = STEPS * count
+    forward = (upwind == 1).astype(jnp.float32)
+    behind, ahead = courant * forward, courant * (1.0 - forward)
+    stay = 1.0 - courant[0] - courant[1] - courant[2] - relaxation
+    rates = jnp.stack([stay, behind[0], ahead[0], behind[1], ahead[1], behind[2], ahead[2], source])
+    heat = heaters[0].astype(jnp.float32).reshape(planes, ny * nz, 1)
+    anywhere, vmem = pl.BlockSpec(memory_space=pl.ANY), pl.BlockSpec(memory_space=pltpu.VMEM)
+    dma = pltpu.SemaphoreType.DMA
+    half, full = jnp.bfloat16, jnp.float32
+    return pl.pallas_call(
+        line_kernel,
+        out_shape=jax.ShapeDtypeStruct(phonons.shape, full),
+        in_specs=[anywhere, vmem, vmem, anywhere],
+        out_specs=anywhere,
+        scratch_shapes=[
+            pltpu.VMEM((planes + 1, ny, nz, width), full),
+            pltpu.VMEM((count, PLANES, ny, nz, width), half),
+            pltpu.VMEM((3, calls, PLANES, ny, nz, width), half),
+            pltpu.VMEM((6, width, width), half),
+            pltpu.VMEM((2, ny + 2, nz, width), full),
+            pltpu.VMEM((2, STEPS, ny, nz, width), half),
+            pltpu.VMEM((2, calls, PLANES, nz, width), half),
+            pltpu.VMEM((PLANES * ny * nz, width), full),
+            dma((5,)),
+            dma((4, calls)),
+            dma((3, calls)),
+            dma((2, calls)),
+            dma((2, calls)),
+            dma((2, STEPS)),
+            dma((2, STEPS)),
+            dma((16,)),
+            dma((16,)),
+            dma((count,)),
+        ],
+        compiler_params=pltpu.CompilerParams(
+            collective_id=0, has_side_effects=True, vmem_limit_bytes=64 * 2**20 - 2**18
+        ),
+    )(phonons, heat, rates, coupling)
 
 
 def shifted(block, axis, distance):
@@ -80,8 +391,9 @@
         P("modes"),
         P("modes", None),
     )
+    on_line = mesh.shape["modes"] == 4 and mesh.shape["cells"] == 8
     return jax.shard_map(
-        per_device,
+        line_device if on_line else per_device,
         mesh=mesh,
         in_specs=placed,
         out_specs=P("cells", None, None, None, "modes"),

time: 520 us -> 370 us (0.71)
  waiting for transfers between devices: 369 us -> 0 us
  Pallas kernels: 0 us -> 356 us
  other arithmetic: 58.1 us -> 3.86 us
  matrix products: 48.2 us -> 0 us
  between operations: 13.8 us -> 0.03 us
  starting transfers between devices: 11 us -> 0 us
  local copies, waits for them, and re-layouts: 19.2 us -> 8.83 us
    all_gather x2 -> x0, waiting for transfers between devices: 358 us -> none  [scatter_term(): gathered = lax.all_gather(rounded, 'modes', axis=1, tiled=True)]
    pallas_call x0 -> x1, Pallas kernels: none -> 356 us  [line_device(): pl.pallas_call(line_kernel, out_shape=jax.ShapeDtypeStruct(phonons.shape,...]
    dot_general x2 -> x0, matrix products: 48.2 us -> none  [scatter_term(): lax.dot_general(gathered, coupling, contract, preferred_element_type=jnp....]
    add x2 -> x0, other arithmetic: 25.2 us -> none  [advect(): transport = transport + courant[2] * (density - upstream_z)]
    another operation x2 -> x0, other arithmetic: 13.1 us -> none
    ppermute x8 -> x0, waiting for transfers between devices: 11.2 us -> none  [shifted(): return lax.ppermute(block, axis, route)]
    ppermute x8 -> x0, starting transfers between devices: 11 us -> none  [shifted(): return lax.ppermute(block, axis, route)]
    scatter-add x8 -> x0, other arithmetic: 10.5 us -> none  [the longest x2 3.2 us: advect(): transport.at[:, -1].add(-courant[1] * jnp.where(forward_y, 0.0, above_y))]
  transfers between devices with their start and end apart: 10 -> 0, of which waited for: 5 -> 0; matrix products, arithmetic and copies ran while one was open for 11% -> 0% of each run, Pallas kernels for 0% -> 0%
where the time goes in v1:
time: 370 us; the launch traced here: 369 us
  Pallas kernels  356 us (96%)
  local copies, waits for them, and re-layouts  8.83 us (2%)
  other arithmetic  3.86 us (1%)
    pallas_call x1, Pallas kernels, line_device(): pl.pallas_call(line_kernel, out_shape=jax.ShapeDtypeStruct(phonons.shape,...  356 us

profile of v1, /device:TPU:0, one launch (start us, length us, event | category | flops | bytes accessed | tf_op | source)
XLA Modules:
  0.0 369.2 jit_solution(14766220087967709097)
XLA Ops:
  0.0 0.7 stack.10
  0.7 0.9 subtract_reduce_fusion
  1.6 0.7 sub.31
  2.3 0.8 subtract_multiply_fusion
  3.1 0.8 broadcast_select_fusion
  3.9 0.7 stack.11.rates
  4.6 0.8 convert_element_type.16
  5.3 1.1 convert_element_type.19.heat
  6.4 356.4 %shard_map.73 = f32[1,8,8,16,1536]{4,3,2,1,0:T(8,128)} custom-call(f32[1,8,8,16,1536]{4,3,2,1,0:T(8,128)} %phonons.1, f32[8,128,1]{2,1,0:T(8,128)} %convert_element_type.19.heat, f32[8,1536]{1,0:T(8,128)} %stack.11.rates, bf16[1536,6144]{1,0:T(8,128)(2,1)} %coupling.1), custom_call_target="tpu_custom_call" | custom-call | tf_op jit(solution)/shard_map/pallas_call | solution.py:290
  362.9 6.3 %copy.10 = f32[1,8,8,16,1536]{4,3,2,1,0:T(8,128)} copy(f32[1,8,8,16,1536]{4,3,2,1,0:T(8,128)} %shard_map.73) | data formatting | bytes 12582912
  (2 shorter events, 0.0 us)

commit v2 on v1

--- a/solution.py
+++ b/solution.py
@@ -9,8 +9,8 @@
 STEPS = 2
 
 PLANES = 1
-TILE = 256
-LENT_AT = 5
+TILE = 768
+LENT_FROM, LENT_TWIN, LENT_AT = 0, 3, 4
 MESH = pl.DeviceIdType.MESH
 
 
@@ -208,6 +208,8 @@
     def _():
         lent_z(0).start()
         lent_z(1).start()
+        lent_z(0).wait_send()
+        lent_z(1).wait_send()
 
     load_density.wait()
 
@@ -223,24 +225,24 @@
     def _(t):
         @pl.when(is_inner)
         def _():
-            @pl.when(t < steps_all)
-            def _():
-                arrived(1, t)
-                relay(t).start()
-
-            @pl.when(t == LENT_AT - 3)
+            @pl.when(t == LENT_FROM)
             def _():
                 for k in range(2):
                     lent_z(k).wait_recv()
                 for q, k in pairs:
                     lent_peer(q, k).start()
 
-            @pl.when(t == LENT_AT - 1)
+            @pl.when(t == LENT_TWIN)
             def _():
                 for q, k in pairs:
                     lent_peer(q, k).wait_recv()
                 for q, k in twins:
                     lent_twin(q, k).start()
+
+            @pl.when(t < steps_all)
+            def _():
+                arrived(1, t)
+                relay(t).start()
 
         @pl.when(t >= 1)
         def _():
@@ -268,11 +270,6 @@
             lent_peer(q, k).wait_send()
         for q, k in twins:
             lent_twin(q, k).wait_send()
-
-    @pl.when(jnp.logical_not(is_inner))
-    def _():
-        lent_z(0).wait_send()
-        lent_z(1).wait_send()
 
 
 def line_device(phonons, heaters, courant, upwind, relaxation, source, coupling):

time: 370 us -> 332 us (0.90)
  Pallas kernels: 356 us -> 319 us
    pallas_call x1, Pallas kernels: 356 us -> 319 us  [line_device(): pl.pallas_call(line_kernel, out_shape=jax.ShapeDtypeStruct(phonons.shape,...]
where the time goes in v2:
time: 332 us
  Pallas kernels  319 us (96%)
  local copies, waits for them, and re-layouts  8.83 us (3%)
  other arithmetic  3.86 us (1%)
    pallas_call x1, Pallas kernels, line_device(): pl.pallas_call(line_kernel, out_shape=jax.ShapeDtypeStruct(phonons.shape,...  319 us

profile of v2, /device:TPU:0, one launch (start us, length us, event | category | flops | bytes accessed | tf_op | source)
XLA Modules:
  0.0 331.8 jit_solution(7353710839752019128)
XLA Ops:
  0.0 0.7 stack.10
  0.7 0.9 subtract_reduce_fusion
  1.6 0.7 sub.31
  2.3 0.8 subtract_multiply_fusion
  3.1 0.8 broadcast_select_fusion
  3.9 0.7 stack.11.rates
  4.6 0.8 convert_element_type.16
  5.3 1.1 convert_element_type.19.heat
  6.4 319.0 %shard_map.73 = f32[1,8,8,16,1536]{4,3,2,1,0:T(8,128)} custom-call(f32[1,8,8,16,1536]{4,3,2,1,0:T(8,128)} %phonons.1, f32[8,128,1]{2,1,0:T(8,128)} %convert_element_type.19.heat, f32[8,1536]{1,0:T(8,128)} %stack.11.rates, bf16[1536,6144]{1,0:T(8,128)(2,1)} %coupling.1), custom_call_target="tpu_custom_call" | custom-call | tf_op jit(solution)/shard_map/pallas_call | solution.py:287
  325.5 6.3 %copy.10 = f32[1,8,8,16,1536]{4,3,2,1,0:T(8,128)} copy(f32[1,8,8,16,1536]{4,3,2,1,0:T(8,128)} %shard_map.73) | data formatting | bytes 12582912
  (2 shorter events, 0.0 us)
